TPU v7x, 256 devices: a whole 4x4x8 slice. The times are simulated.
256 devices in a mesh: rows: 64 (over y_lo, z, x), blk: 4 (over y_hi, core).
Axes of the slice: x: 4, y: 4 (y_hi: 2, y_lo: 2; y = y_hi * 2 + y_lo), z: 8, core: 2. Of those that a mesh axis runs over, the one named last changes fastest.
Arguments:
- block_weight: bfloat16 [64, 4, 4, 64, 128, 128], P('rows', 'blk'), may hold values from 0.049804688 to 50
- block_row: int32 [64, 4, 4, 64], P('rows', 'blk'), may hold values from 0 to 15, as said below
- block_col: int32 [64, 4, 4, 64], P('rows', 'blk'), may hold values from 0 to 7, as said below
- block_count: int32 [64, 4, 4], P('rows', 'blk'), may hold values from 1 to 64, as said below
- block_samples: int32 [64, 4, 4, 64], P('rows', 'blk'), may hold values from 1 to 8
- row_degree: float32 [64, 4, 2048], P('rows', 'blk'), may hold values from 0.125 to 8
- col_degree: float32 [4, 1024], P('blk', 'rows'), may hold values from 1 to 8
- test_matrix: bfloat16 [4, 1024, 128], P('blk', 'rows'), may hold values from -6 to 6
Outputs:
- basis: float32 [64, 4, 2048, 128], P('rows', 'blk')
- triangle: float32 [128, 128], replicated
Inputs may be any that keep to these rules, and one draw needn't show every extreme that they name: Within one band and slab, the slots k < 64 hold distinct (block_row, block_col) pairs. `block_col`: see block_row: pairs are distinct within one band and slab. `block_count`: some band and slab has all 64 slots live in every draw.
All inputs are finite; a program needn't handle non-finite values.
Results may differ from a plain program's by a relative error of at most 0.0065.
Values may be sent and summed in bfloat16 or wider, within the bound.
A program may use at most 64 MiB of HBM per device.

v0:
```python
import jax
import jax.numpy as jnp
from jax import lax
from jax.sharding import PartitionSpec as P

scale_factor = 16.0


def passed_along(block, axis, distance):
    devices = range(lax.axis_size(axis))
    route = [((i - distance) % len(devices), i) for i in devices]
    return lax.ppermute(block, axis, route)


def tile_update(
    running, weights, rows_idx, cols_idx, live_count, samples, row_deg, slab_rows, slab_deg
):
    block_edge = weights.shape[-1]
    capacity = weights.shape[0]
    band_blocks = running.shape[0]
    slab_blocks = slab_rows.shape[0] // block_edge
    slab_tiles = slab_rows.reshape(slab_blocks, block_edge, slab_rows.shape[1])
    picked = slab_tiles[cols_idx]
    col_d = slab_deg.reshape(slab_blocks, block_edge)[cols_idx]
    row_d = row_deg.reshape(band_blocks, block_edge)[rows_idx]
    scaled_ratio = (
        scale_factor
        * weights.astype(jnp.float32)
        / (samples.astype(jnp.float32)[:, None, None] * row_d[:, :, None] * col_d[:, None, :])
    )
    entries = jnp.log(jnp.maximum(scaled_ratio, 1.0)).astype(jnp.bfloat16)
    products = jnp.einsum("kij,kjc->kic", entries, picked, preferred_element_type=jnp.float32)
    alive_mask = (jnp.arange(capacity, dtype=jnp.int32) < live_count).astype(jnp.float32)
    chooser = (rows_idx[None, :] == jnp.arange(band_blocks, dtype=jnp.int32)[:, None]).astype(
        jnp.float32
    ) * alive_mask[None, :]
    return running + jnp.einsum("rk,kic->ric", chooser, products, precision=lax.Precision.HIGHEST)


def body(
    block_weight,
    block_row,
    block_col,
    block_count,
    block_samples,
    row_degree,
    col_degree,
    test_matrix,
):
    loop_size = lax.axis_size("blk")
    position = lax.axis_index("blk")
    weights_all = block_weight[0, 0]
    rows_all = block_row[0, 0]
    cols_all = block_col[0, 0]
    counts_all = block_count[0, 0]
    samples_all = block_samples[0, 0]
    row_deg = row_degree[0, 0]
    block_edge = weights_all.shape[-1]
    band_blocks = row_deg.shape[0] // block_edge
    running = jnp.zeros((band_blocks, block_edge, test_matrix.shape[2]), jnp.float32)
    piece_pair = (test_matrix, col_degree)
    for t in range(loop_size):
        if t > 0:
            piece_pair = (
                passed_along(piece_pair[0], "blk", 1),
                passed_along(piece_pair[1].astype(jnp.bfloat16), "blk", 1).astype(jnp.float32),
            )
        slab_rows, slab_deg = (
            lax.all_gather(piece_pair[0], "rows", axis=1, tiled=True),
            lax.all_gather(piece_pair[1].astype(jnp.bfloat16), "rows", axis=1, tiled=True).astype(
                jnp.float32
            ),
        )
        slab_index = (position - t) % loop_size
        apply_slab_rows = slab_rows[0]
        apply_slab_deg = slab_deg[0]
        slab_index = jnp.asarray(slab_index)
        running = tile_update(
            running,
            lax.dynamic_index_in_dim(weights_all, slab_index, 0, keepdims=False),
            lax.dynamic_index_in_dim(rows_all, slab_index, 0, keepdims=False),
            lax.dynamic_index_in_dim(cols_all, slab_index, 0, keepdims=False),
            lax.dynamic_index_in_dim(counts_all, slab_index, 0, keepdims=False),
            lax.dynamic_index_in_dim(samples_all, slab_index, 0, keepdims=False),
            row_deg,
            apply_slab_rows,
            apply_slab_deg,
        )
    flat_rows = running.reshape(band_blocks * block_edge, running.shape[2])
    gram_local = jnp.dot(
        flat_rows.T, flat_rows, precision=lax.Precision.HIGHEST, preferred_element_type=jnp.float32
    )
    gram_total = lax.psum(gram_local, ("rows", "blk"))
    lower_factor = jnp.linalg.cholesky(gram_total)
    total_rows = flat_rows.shape[0] * lax.axis_size("rows") * loop_size
    root = jnp.sqrt(jnp.float32(total_rows))
    basis_rows = (
        lax.linalg.triangular_solve(
            lower_factor, flat_rows, left_side=False, lower=True, transpose_a=True
        )
        * root
    )
    return (basis_rows.reshape(1, 1, flat_rows.shape[0], flat_rows.shape[1]), lower_factor.T / root)


def solution(mesh):
    placed = (
        P("rows", "blk", None, None, None, None),
        P("rows", "blk", None, None),
        P("rows", "blk", None, None),
        P("rows", "blk", None),
        P("rows", "blk", None, None),
        P("rows", "blk", None),
        P("blk", "rows"),
        P("blk", "rows", None),
    )
    return jax.shard_map(
        body,
        mesh=mesh,
        in_specs=placed,
        out_specs=(P("rows", "blk", None, None), P()),
        check_vma=False,
    )
```

profile of v0, /device:TPU:1, one launch (start us, length us, event | category | flops | bytes accessed | tf_op | source)
XLA Modules:
  0.0 1118.6 jit_solution(2050559915229179514)
XLA Ops:
  7.2 4.4 collective-permute-start.1
  12.3 132.2 %all_gather.25 = bf16[1,1024,128]{2,1,0:T(8,128)(2,1)S(1)} all-gather(bf16[1,16,128]{2,1,0:T(8,128)(2,1)} %param.15), channel_id=1, replica_groups=mesh['rows'=64,'blk'=4] {'rows'}, dimensions={1}, use_global_device_ids=true | all-gather | bytes 266240 | tf_op jit(solution)/shard_map/all_gather | solution.py:69
  158.6 29.4 %collective-permute-start.2 = (bf16[1,16]{1,0:T(2,128)(2,1)S(1)}, bf16[1,16]{1,0:T(2,128)(2,1)S(1)}, u32[]{:S(2)}, u32[]{:S(2)}) collective-permute-start(bf16[1,16]{1,0:T(2,128)(2,1)S(1)} %collective-permute-done), channel_id=1, source_target_pairs={{3,0},{0,1},{1,2},{2,3},{7,4},{4,5},{5,6},{6,7},{11,8},{8,9},{9,10... | collective-permute-start | bytes 104 | tf_op jit(solution)/shard_map/ppermute | solution.py:12
  188.9 3.8 collective-permute-start.4
  193.6 127.1 %all-reduce.4 = (bf16[1024]{0:T(1024)(128)(2,1)S(1)}, bf16[1024]{0:T(1024)(128)(2,1)S(1)}, bf16[1024]{0:T(1024)(128)(2,1)S(1)}, bf16[1024]{0:T(1024)(128)(2,1)S(1)}) all-reduce(bf16[1024]{0:T(1024)(128)(2,1)S(1)} %dynamic-update-slice.4, bf16[1024]{0:T(1024)(128)(2,1)S(1)} %dynamic-update-slice.3, ...), channel_id=1, replica_groups=mesh['rows'=64,'blk'=4] {'rows'}, use_global_device_ids=true, to_apply=%add.1 | all-reduce | flops 4096 | bytes 16384
  321.4 4.1 fusion.21
  327.3 124.8 %all_gather.27 = bf16[1,1024,128]{2,1,0:T(8,128)(2,1)S(1)} all-gather(bf16[1,16,128]{2,1,0:T(8,128)(2,1)S(1)} %collective-permute-done.1), channel_id=1, replica_groups=mesh['rows'=64,'blk'=4] {'rows'}, dimensions={1}, use_global_device_ids=true | all-gather | bytes 266240 | tf_op jit(solution)/shard_map/all_gather | solution.py:69
  453.1 3.6 fusion.23
  456.7 4.4 fusion.16
  461.0 60.1 %collective-permute-start.3 = (bf16[1,16,128]{2,1,0:T(8,128)(2,1)S(1)}, bf16[1,16,128]{2,1,0:T(8,128)(2,1)S(1)}, u32[]{:S(2)}, u32[]{:S(2)}) collective-permute-start(bf16[1,16,128]{2,1,0:T(8,128)(2,1)S(1)} %collective-permute-done.1), channel_id=1, source_target_pairs={{3,0},{0,1},{1,2},{2,3},{7,4},{4,5},{5,6},{6,7},{11,8},{8,9},{9,10... | collective-permute-start | bytes 12296 | tf_op jit(solution)/shard_map/ppermute | solution.py:12
  521.1 4.4 fusion.49
  525.5 124.0 %all_gather.29 = bf16[1,1024,128]{2,1,0:T(8,128)(2,1)S(1)} all-gather(bf16[1,16,128]{2,1,0:T(8,128)(2,1)S(1)} %collective-permute-done.3), channel_id=1, replica_groups=mesh['rows'=64,'blk'=4] {'rows'}, dimensions={1}, use_global_device_ids=true | all-gather | bytes 266240 | tf_op jit(solution)/shard_map/all_gather | solution.py:69
  650.6 3.6 fusion.25
  654.2 27.5 %collective-permute-start.5 = (bf16[1,16,128]{2,1,0:T(8,128)(2,1)S(1)}, bf16[1,16,128]{2,1,0:T(8,128)(2,1)S(1)}, u32[]{:S(2)}, u32[]{:S(2)}) collective-permute-start(bf16[1,16,128]{2,1,0:T(8,128)(2,1)S(1)} %copy-done.3), channel_id=1, source_target_pairs={{3,0},{0,1},{1,2},{2,3},{7,4},{4,5},{5,6},{6,7},{11,8},{8,9},{9,10... | collective-permute-start | bytes 12296 | tf_op jit(solution)/shard_map/ppermute | solution.py:12
  681.8 4.4 fusion.52
  686.2 125.7 %all_gather.31 = bf16[1,1024,128]{2,1,0:T(8,128)(2,1)S(1)} all-gather(bf16[1,16,128]{2,1,0:T(8,128)(2,1)S(1)} %collective-permute-done.5), channel_id=1, replica_groups=mesh['rows'=64,'blk'=4] {'rows'}, dimensions={1}, use_global_device_ids=true | all-gather | bytes 266240 | tf_op jit(solution)/shard_map/all_gather | solution.py:69
  811.9 2.1 gather_fusion.11
  814.0 3.3 fusion.27
  817.4 4.4 fusion.55
  821.8 2.5 convolution_bitcast_fusion
  824.7 259.5 %all-reduce.7.cloned.1.call-done = f32[128,128]{0,1:T(8,128)} async-done(((f32[128,128]{0,1:T(8,128)}), f32[128,128]{0,1:T(8,128)}) %all-reduce.7.cloned.1.call-update) | async-done | bytes 65552 | tf_op jit(solution)/shard_map/psum | solution.py:93
  1086.0 11.7 %cholesky.16 = f32[128,128]{1,0:T(8,128)S(1)} custom-call(f32[128,128]{1,0:T(8,128)S(1)} %fusion.59), custom_call_target="Cholesky" | custom-call | tf_op jit(solution)/shard_map/jit(cholesky)/cholesky | solution.py:94
  1099.1 9.8 custom-call.6
  1109.6 1.9 fusion.20
  (77 shorter events, 24.5 us)
Async XLA Ops:
  7.2 142.5 %copy-start = (f32[1,1,2048]{2,1,0:T(1,128)S(1)}, f32[1,1,2048]{2,1,0:T(1,128)}, u32[]{:S(2)}) copy-start(f32[1,1,2048]{2,1,0:T(1,128)} %param.13) | copy-start | bytes 24580
  7.2 1077.0 %all-reduce.7.cloned.1.call-start = ((), (), s32[]{:S(2)}) async-start(), calls=%async_computation | async-start | bytes 131072 | tf_op jit(solution)/shard_map/psum | solution.py:93
  7.2 320.1 %collective-permute-start.1 = (bf16[1,16,128]{2,1,0:T(8,128)(2,1)}, bf16[1,16,128]{2,1,0:T(8,128)(2,1)S(1)}, u32[]{:S(2)}, u32[]{:S(2)}) collective-permute-start(bf16[1,16,128]{2,1,0:T(8,128)(2,1)} %param.15), channel_id=1, source_target_pairs={{3,0},{0,1},{1,2},{2,3},{7,4},{4,5},{5,6},{6,7},{11,8},{8,9},{9,10... | collective-permute-start | bytes 12296 | tf_op jit(solution)/shard_map/ppermute | solution.py:12
  12.3 146.1 %collective-permute-start = (bf16[1,16]{1,0:T(2,128)(2,1)S(1)}, bf16[1,16]{1,0:T(2,128)(2,1)S(1)}, u32[]{:S(2)}, u32[]{:S(2)}) collective-permute-start(bf16[1,16]{1,0:T(2,128)(2,1)S(1)} %get-tuple-element.33), channel_id=1, source_target_pairs={{3,0},{0,1},{1,2},{2,3},{7,4},{4,5},{5,6},{6,7},{11,8},{8,9},{9,10... | collective-permute-start | bytes 104 | tf_op jit(solution)/shard_map/ppermute | solution.py:12
  158.6 30.1 %collective-permute-start.2 = (bf16[1,16]{1,0:T(2,128)(2,1)S(1)}, bf16[1,16]{1,0:T(2,128)(2,1)S(1)}, u32[]{:S(2)}, u32[]{:S(2)}) collective-permute-start(bf16[1,16]{1,0:T(2,128)(2,1)S(1)} %collective-permute-done), channel_id=1, source_target_pairs={{3,0},{0,1},{1,2},{2,3},{7,4},{4,5},{5,6},{6,7},{11,8},{8,9},{9,10... | collective-permute-start | bytes 104 | tf_op jit(solution)/shard_map/ppermute | solution.py:12
  188.9 4.5 collective-permute-start.4
  456.7 64.4 %copy-start.1 = (f32[64,128,128]{2,1,0:T(8,128)S(1)}, f32[64,128,128]{2,1,0:T(8,128)}, u32[]{:S(2)}) copy-start(f32[64,128,128]{2,1,0:T(8,128)} %fusion.21) | copy-start | bytes 12582916
  461.0 64.5 %collective-permute-start.3 = (bf16[1,16,128]{2,1,0:T(8,128)(2,1)S(1)}, bf16[1,16,128]{2,1,0:T(8,128)(2,1)S(1)}, u32[]{:S(2)}, u32[]{:S(2)}) collective-permute-start(bf16[1,16,128]{2,1,0:T(8,128)(2,1)S(1)} %collective-permute-done.1), channel_id=1, source_target_pairs={{3,0},{0,1},{1,2},{2,3},{7,4},{4,5},{5,6},{6,7},{11,8},{8,9},{9,10... | collective-permute-start | bytes 12296 | tf_op jit(solution)/shard_map/ppermute | solution.py:12
  525.5 124.0 %copy-start.2 = (bf16[1,16,128]{2,1,0:T(8,128)(2,1)}, bf16[1,16,128]{2,1,0:T(8,128)(2,1)S(1)}, u32[]{:S(2)}) copy-start(bf16[1,16,128]{2,1,0:T(8,128)(2,1)S(1)} %collective-permute-done.3) | copy-start | bytes 12292
  650.5 3.7 copy-start.3
  650.5 31.2 %copy-start.5 = (s32[64]{0:T(128)S(1)}, s32[64]{0:T(128)}, u32[]{:S(2)}) copy-start(s32[64]{0:T(128)} %get-tuple-element.15) | copy-start | bytes 772
  650.5 31.2 %copy-start.7 = (f32[64]{0:T(128)S(1)}, f32[64]{0:T(128)}, u32[]{:S(2)}) copy-start(f32[64]{0:T(128)} %compare_convert_fusion.1) | copy-start | bytes 772
  654.2 32.0 %collective-permute-start.5 = (bf16[1,16,128]{2,1,0:T(8,128)(2,1)S(1)}, bf16[1,16,128]{2,1,0:T(8,128)(2,1)S(1)}, u32[]{:S(2)}, u32[]{:S(2)}) collective-permute-start(bf16[1,16,128]{2,1,0:T(8,128)(2,1)S(1)} %copy-done.3), channel_id=1, source_target_pairs={{3,0},{0,1},{1,2},{2,3},{7,4},{4,5},{5,6},{6,7},{11,8},{8,9},{9,10... | collective-permute-start | bytes 12296 | tf_op jit(solution)/shard_map/ppermute | solution.py:12
  814.0 3.4 copy-start.4
  814.0 3.4 copy-start.6
Sparse Core Ops, SparseCore 0:
  824.5 259.6 all-reduce.6
where the time goes:
time: 1120 us
  blocking collectives  634 us (57%)
  waiting for transfers between devices  261 us (23%)
  starting transfers between devices  125 us (11%)
  matrix products  36.7 us (3%)
  other arithmetic  29.9 us (3%)
  local copies, waits for them, and re-layouts  16.8 us (2%)
  between operations  15.2 us (1%)
    all_gather x4, blocking collectives, body(): lax.all_gather(piece_pair[0], 'rows', axis=1, tiled=True)  507 us
    psum x1, waiting for transfers between devices, body(): gram_total = lax.psum(gram_local, ('rows', 'blk'))  260 us
    unnamed x1, blocking collectives  127 us
    ppermute x6, starting transfers between devices, passed_along(): return lax.ppermute(block, axis, route)  125 us
  transfers between devices with their start and end apart: 7, of which 3 were waited for; matrix products, arithmetic and copies ran while one was open for 3% of the time, Pallas kernels for 0%

commit v1 on v0

--- a/solution.py
+++ b/solution.py
@@ -90,7 +90,7 @@
     gram_local = jnp.dot(
         flat_rows.T, flat_rows, precision=lax.Precision.HIGHEST, preferred_element_type=jnp.float32
     )
-    gram_total = lax.psum(gram_local, ("rows", "blk"))
+    gram_total = jnp.sum(lax.all_gather(gram_local, ("rows", "blk")), axis=0)
     lower_factor = jnp.linalg.cholesky(gram_total)
     total_rows = flat_rows.shape[0] * lax.axis_size("rows") * loop_size
     root = jnp.sqrt(jnp.float32(total_rows))

time: 1120 us -> 1320 us (1.18)
  waiting for transfers between devices: 261 us -> 448 us
    all_gather x0 -> x1, waiting for transfers between devices: none -> 446 us  [body(): gram_total = jnp.sum(lax.all_gather(gram_local, ('rows', 'blk')), axis=0)]
    psum x1 -> x0, waiting for transfers between devices: 260 us -> none  [body(): gram_total = lax.psum(gram_local, ('rows', 'blk'))]
  transfers between devices with their start and end apart: 7 -> 7, of which waited for: 3 -> 3; matrix products, arithmetic and copies ran while one was open for 3% -> 2% of each run, Pallas kernels for 0% -> 0%
where the time goes in v1:
time: 1320 us; the launch traced here: 1310 us
  blocking collectives  634 us (48%)
  waiting for transfers between devices  448 us (34%)
  starting transfers between devices  125 us (9%)
  matrix products  36.8 us (3%)
  other arithmetic  36 us (3%)
  local copies, waits for them, and re-layouts  15.8 us (1%)
  between operations  15.3 us (1%)
    all_gather x4, blocking collectives, body(): lax.all_gather(piece_pair[0], 'rows', axis=1, tiled=True)  507 us
    all_gather x1, waiting for transfers between devices, body(): gram_total = jnp.sum(lax.all_gather(gram_local, ('rows', 'blk')), axis=0)  446 us
    unnamed x1, blocking collectives  127 us
    ppermute x6, starting transfers between devices, passed_along(): return lax.ppermute(block, axis, route)  125 us
  transfers between devices with their start and end apart: 7, of which 3 were waited for; matrix products, arithmetic and copies ran while one was open for 2% of the time, Pallas kernels for 0%

profile of v1, /device:TPU:1, one launch (start us, length us, event | category | flops | bytes accessed | tf_op | source)
XLA Modules:
  0.0 1310.8 jit_solution(8372121605929073758)
XLA Ops:
  7.9 4.3 collective-permute-start
  12.2 132.2 %all_gather.31 = bf16[1,1024,128]{2,1,0:T(8,128)(2,1)S(1)} all-gather(bf16[1,16,128]{2,1,0:T(8,128)(2,1)} %param.15), channel_id=1, replica_groups=mesh['rows'=64,'blk'=4] {'rows'}, dimensions={1}, use_global_device_ids=true | all-gather | bytes 266240 | tf_op jit(solution)/shard_map/all_gather | solution.py:69
  158.7 29.4 %collective-permute-start.2 = (bf16[1,16]{1,0:T(2,128)(2,1)S(1)}, bf16[1,16]{1,0:T(2,128)(2,1)S(1)}, u32[]{:S(2)}, u32[]{:S(2)}) collective-permute-start(bf16[1,16]{1,0:T(2,128)(2,1)S(1)} %collective-permute-done), channel_id=1, source_target_pairs={{3,0},{0,1},{1,2},{2,3},{7,4},{4,5},{5,6},{6,7},{11,8},{8,9},{9,10... | collective-permute-start | bytes 104 | tf_op jit(solution)/shard_map/ppermute | solution.py:12
  189.0 3.8 collective-permute-start.4
  193.7 127.1 %all-reduce.4 = (bf16[1024]{0:T(1024)(128)(2,1)S(1)}, bf16[1024]{0:T(1024)(128)(2,1)S(1)}, bf16[1024]{0:T(1024)(128)(2,1)S(1)}, bf16[1024]{0:T(1024)(128)(2,1)S(1)}) all-reduce(bf16[1024]{0:T(1024)(128)(2,1)S(1)} %dynamic-update-slice.4, bf16[1024]{0:T(1024)(128)(2,1)S(1)} %dynamic-update-slice.3, ...), channel_id=1, replica_groups=mesh['rows'=64,'blk'=4] {'rows'}, use_global_device_ids=true, to_apply=%add.1 | all-reduce | flops 4096 | bytes 16384
  321.4 4.1 fusion.21
  327.3 124.9 %all_gather.33 = bf16[1,1024,128]{2,1,0:T(8,128)(2,1)S(1)} all-gather(bf16[1,16,128]{2,1,0:T(8,128)(2,1)S(1)} %collective-permute-done.1), channel_id=1, replica_groups=mesh['rows'=64,'blk'=4] {'rows'}, dimensions={1}, use_global_device_ids=true | all-gather | bytes 266240 | tf_op jit(solution)/shard_map/all_gather | solution.py:69
  453.1 3.6 fusion.23
  456.8 4.4 fusion.16
  461.1 60.1 %collective-permute-start.3 = (bf16[1,16,128]{2,1,0:T(8,128)(2,1)S(1)}, bf16[1,16,128]{2,1,0:T(8,128)(2,1)S(1)}, u32[]{:S(2)}, u32[]{:S(2)}) collective-permute-start(bf16[1,16,128]{2,1,0:T(8,128)(2,1)S(1)} %collective-permute-done.1), channel_id=1, source_target_pairs={{3,0},{0,1},{1,2},{2,3},{7,4},{4,5},{5,6},{6,7},{11,8},{8,9},{9,10... | collective-permute-start | bytes 12296 | tf_op jit(solution)/shard_map/ppermute | solution.py:12
  521.2 4.4 fusion.49
  525.6 124.0 %all_gather.35 = bf16[1,1024,128]{2,1,0:T(8,128)(2,1)S(1)} all-gather(bf16[1,16,128]{2,1,0:T(8,128)(2,1)S(1)} %collective-permute-done.3), channel_id=1, replica_groups=mesh['rows'=64,'blk'=4] {'rows'}, dimensions={1}, use_global_device_ids=true | all-gather | bytes 266240 | tf_op jit(solution)/shard_map/all_gather | solution.py:69
  650.6 3.6 fusion.25
  654.3 27.5 %collective-permute-start.5 = (bf16[1,16,128]{2,1,0:T(8,128)(2,1)S(1)}, bf16[1,16,128]{2,1,0:T(8,128)(2,1)S(1)}, u32[]{:S(2)}, u32[]{:S(2)}) collective-permute-start(bf16[1,16,128]{2,1,0:T(8,128)(2,1)S(1)} %copy-done.3), channel_id=1, source_target_pairs={{3,0},{0,1},{1,2},{2,3},{7,4},{4,5},{5,6},{6,7},{11,8},{8,9},{9,10... | collective-permute-start | bytes 12296 | tf_op jit(solution)/shard_map/ppermute | solution.py:12
  681.8 4.4 fusion.52
  686.3 125.7 %all_gather.37 = bf16[1,1024,128]{2,1,0:T(8,128)(2,1)S(1)} all-gather(bf16[1,16,128]{2,1,0:T(8,128)(2,1)S(1)} %collective-permute-done.5), channel_id=1, replica_groups=mesh['rows'=64,'blk'=4] {'rows'}, dimensions={1}, use_global_device_ids=true | all-gather | bytes 266240 | tf_op jit(solution)/shard_map/all_gather | solution.py:69
  812.0 2.1 gather_fusion.11
  814.1 3.4 fusion.27
  817.5 4.4 fusion.55
  821.9 2.5 convolution_bitcast_fusion
  824.8 446.4 %all-gather.3.cloned.1.call-done = f32[32768,128]{1,0:T(8,128)} async-done(((f32[128,128]{1,0:T(8,128)}), f32[32768,128]{1,0:T(8,128)}) %all-gather.3.cloned.1.call-update) | async-done | bytes 16777232 | tf_op jit(solution)/shard_map/all_gather | solution.py:93
  1271.2 6.6 reduce_sum.9
  1277.9 11.7 cholesky.16
  1291.7 10.0 custom-call.6
  (78 shorter events, 24.9 us)
Async XLA Ops:
  7.2 145.4 %copy-start = (f32[1,1,2048]{2,1,0:T(1,128)S(1)}, f32[1,1,2048]{2,1,0:T(1,128)}, u32[]{:S(2)}) copy-start(f32[1,1,2048]{2,1,0:T(1,128)} %param.13) | copy-start | bytes 24580
  7.2 1264.0 %all-gather.3.cloned.1.call-start = ((), (), s32[]{:S(2)}) async-start(), calls=%async_computation | async-start | bytes 16842752 | tf_op jit(solution)/shard_map/all_gather | solution.py:93
  7.9 150.5 %collective-permute-start = (bf16[1,16]{1,0:T(2,128)(2,1)S(1)}, bf16[1,16]{1,0:T(2,128)(2,1)S(1)}, u32[]{:S(2)}, u32[]{:S(2)}) collective-permute-start(bf16[1,16]{1,0:T(2,128)(2,1)S(1)} %get-tuple-element.35), channel_id=1, source_target_pairs={{3,0},{0,1},{1,2},{2,3},{7,4},{4,5},{5,6},{6,7},{11,8},{8,9},{9,10... | collective-permute-start | bytes 104 | tf_op jit(solution)/shard_map/ppermute | solution.py:12
  12.2 315.1 %collective-permute-start.1 = (bf16[1,16,128]{2,1,0:T(8,128)(2,1)}, bf16[1,16,128]{2,1,0:T(8,128)(2,1)S(1)}, u32[]{:S(2)}, u32[]{:S(2)}) collective-permute-start(bf16[1,16,128]{2,1,0:T(8,128)(2,1)} %param.15), channel_id=1, source_target_pairs={{3,0},{0,1},{1,2},{2,3},{7,4},{4,5},{5,6},{6,7},{11,8},{8,9},{9,10... | collective-permute-start | bytes 12296 | tf_op jit(solution)/shard_map/ppermute | solution.py:12
  158.7 30.1 %collective-permute-start.2 = (bf16[1,16]{1,0:T(2,128)(2,1)S(1)}, bf16[1,16]{1,0:T(2,128)(2,1)S(1)}, u32[]{:S(2)}, u32[]{:S(2)}) collective-permute-start(bf16[1,16]{1,0:T(2,128)(2,1)S(1)} %collective-permute-done), channel_id=1, source_target_pairs={{3,0},{0,1},{1,2},{2,3},{7,4},{4,5},{5,6},{6,7},{11,8},{8,9},{9,10... | collective-permute-start | bytes 104 | tf_op jit(solution)/shard_map/ppermute | solution.py:12
  189.0 4.5 collective-permute-start.4
  456.8 64.4 %copy-start.1 = (f32[64,128,128]{2,1,0:T(8,128)S(1)}, f32[64,128,128]{2,1,0:T(8,128)}, u32[]{:S(2)}) copy-start(f32[64,128,128]{2,1,0:T(8,128)} %fusion.21) | copy-start | bytes 12582916
  461.1 64.5 %collective-permute-start.3 = (bf16[1,16,128]{2,1,0:T(8,128)(2,1)S(1)}, bf16[1,16,128]{2,1,0:T(8,128)(2,1)S(1)}, u32[]{:S(2)}, u32[]{:S(2)}) collective-permute-start(bf16[1,16,128]{2,1,0:T(8,128)(2,1)S(1)} %collective-permute-done.1), channel_id=1, source_target_pairs={{3,0},{0,1},{1,2},{2,3},{7,4},{4,5},{5,6},{6,7},{11,8},{8,9},{9,10... | collective-permute-start | bytes 12296 | tf_op jit(solution)/shard_map/ppermute | solution.py:12
  525.6 124.1 %copy-start.2 = (bf16[1,16,128]{2,1,0:T(8,128)(2,1)}, bf16[1,16,128]{2,1,0:T(8,128)(2,1)S(1)}, u32[]{:S(2)}) copy-start(bf16[1,16,128]{2,1,0:T(8,128)(2,1)S(1)} %collective-permute-done.3) | copy-start | bytes 12292
  650.6 3.7 copy-start.3
  650.6 31.2 %copy-start.5 = (s32[64]{0:T(128)S(1)}, s32[64]{0:T(128)}, u32[]{:S(2)}) copy-start(s32[64]{0:T(128)} %get-tuple-element.17) | copy-start | bytes 772
  650.6 31.2 %copy-start.7 = (f32[64]{0:T(128)S(1)}, f32[64]{0:T(128)}, u32[]{:S(2)}) copy-start(f32[64]{0:T(128)} %compare_convert_fusion.1) | copy-start | bytes 772
  654.3 32.0 %collective-permute-start.5 = (bf16[1,16,128]{2,1,0:T(8,128)(2,1)S(1)}, bf16[1,16,128]{2,1,0:T(8,128)(2,1)S(1)}, u32[]{:S(2)}, u32[]{:S(2)}) collective-permute-start(bf16[1,16,128]{2,1,0:T(8,128)(2,1)S(1)} %copy-done.3), channel_id=1, source_target_pairs={{3,0},{0,1},{1,2},{2,3},{7,4},{4,5},{5,6},{6,7},{11,8},{8,9},{9,10... | collective-permute-start | bytes 12296 | tf_op jit(solution)/shard_map/ppermute | solution.py:12
  814.1 3.4 copy-start.4
  814.1 3.4 copy-start.6
Sparse Core Ops, SparseCore 0:
  824.6 446.5 all-gather.2
